TPU v7x, 1024 devices: a whole 8x8x8 slice. The times are simulated.
1024 devices in a mesh: section: 16 (over y, x_lo), seqtp: 64 (over x_hi, z, core).
Axes of the slice: x: 8 (x_hi: 4, x_lo: 2; x = x_hi * 2 + x_lo), y: 8, z: 8, core: 2. Of those that a mesh axis runs over, the one named last changes fastest.
Arguments:
- saved_in: bfloat16 [16, 4, 128, 4096], P('section', None, 'seqtp'), may hold values from -40 to 40
- grad_in: bfloat16 [16, 128, 4096], P('section', 'seqtp'), may hold values from -6 to 6
- slot_table: int32 [16], P('section'), may hold values from 0 to 3
- gain: bfloat16 [16, 4096], P('section'), may hold values from 0.099609375 to 1.8984375
- w_gate: bfloat16 [4096, 24576], P(None, 'seqtp'), may hold values from -0.09375 to 0.09375
- w_up: bfloat16 [4096, 24576], P(None, 'seqtp'), may hold values from -0.09375 to 0.09375
- w_down: bfloat16 [24576, 4096], P('seqtp'), may hold values from -0.0390625 to 0.0390625
Outputs:
- grad_prev: bfloat16 [16, 128, 4096], P('section', 'seqtp')
All inputs are finite; a program needn't handle non-finite values.
Results may differ from a plain program's by a relative error of at most 0.0052.
Values may be sent and summed in bfloat16 or wider, within the bound.
A program may use at most 64 MiB of HBM per device.

v0:
```python
import jax
import jax.numpy as jnp
from jax import lax
from jax.sharding import PartitionSpec as P

EPS = 1e-05


def joined_along(blocks, dim):
    blocks = jnp.moveaxis(blocks, 0, dim)
    lengths = blocks.shape
    return blocks.reshape(*lengths[:dim], lengths[dim] * lengths[dim + 1], *lengths[dim + 2 :])


def copy_for_each(x, axis):
    length = lax.axis_size(axis)
    return lax.all_to_all(jnp.broadcast_to(x[None], (length, *x.shape)), axis, 0, 0, tiled=True)


def gathered_copies(x, axis, dim):
    return joined_along(copy_for_each(x, axis), dim)


def in_blocks(x, dim, length):
    lengths = x.shape
    blocks = x.reshape(*lengths[:dim], length, lengths[dim] // length, *lengths[dim + 1 :])
    return jnp.moveaxis(blocks, dim, 0)


def sum_at_owner(x, axis, dim):
    blocks = in_blocks(x, dim, lax.axis_size(axis))
    arrived = lax.all_to_all(blocks, axis, split_axis=0, concat_axis=0, tiled=True)
    return arrived.sum(axis=0)


def passed_along(x, axis, by):
    length = lax.axis_size(axis)
    return lax.ppermute(x, axis, [(i, (i + by) % length) for i in range(length)])


def rms_norm(values, gain_vec):
    wide = values.astype(jnp.float32)
    recip = lax.rsqrt(jnp.mean(wide * wide, axis=-1, keepdims=True) + EPS)
    return ((wide * recip * gain_vec).astype(jnp.bfloat16), recip)


def transposed(left, weight):
    return lax.dot_general(
        left, weight, (((1,), (1,)), ((), ())), preferred_element_type=jnp.float32
    )


def on_device(saved_in, grad_in, slot_table, gain, w_gate, w_up, w_down):
    cotangent = grad_in[0]
    gain_vec = gain[0].astype(jnp.float32)
    behind = lax.dynamic_index_in_dim(saved_in[0], slot_table[0], 0, keepdims=False)
    normed_b, recip_b = rms_norm(behind, gain_vec)
    width = w_gate.shape[1]
    paired = jnp.stack([normed_b, cotangent])
    piece = gathered_copies(paired, "seqtp", 1)
    gate_b = jnp.dot(piece[0], w_gate, preferred_element_type=jnp.float32)
    up_b = jnp.dot(piece[0], w_up, preferred_element_type=jnp.float32)
    d_hidden = transposed(piece[1], w_down)
    probe = jax.nn.sigmoid(gate_b)
    d_gate = (d_hidden * up_b * probe * (1.0 + gate_b * (1.0 - probe))).astype(jnp.bfloat16)
    d_up = (d_hidden * gate_b * probe).astype(jnp.bfloat16)
    d_both = jnp.concatenate([d_gate, d_up], axis=1)
    grad_sum = sum_at_owner(
        transposed(d_both[:, :width], w_gate) + transposed(d_both[:, width:], w_up), "seqtp", 0
    )
    scaled = gain_vec * grad_sum
    unit = behind.astype(jnp.float32) * recip_b
    grad_x = cotangent.astype(jnp.float32) + recip_b * (
        scaled - unit * jnp.mean(scaled * unit, axis=-1, keepdims=True)
    )
    grad_x = grad_x.astype(jnp.bfloat16)
    grad_prev = passed_along(grad_x, "section", -1)
    return grad_prev[None]


def solution(mesh):
    return jax.shard_map(
        on_device,
        mesh=mesh,
        in_specs=(
            P("section", None, "seqtp", None),
            P("section", "seqtp", None),
            P("section"),
            P("section", None),
            P(None, "seqtp"),
            P(None, "seqtp"),
            P("seqtp", None),
        ),
        out_specs=P("section", "seqtp", None),
        check_vma=False,
    )
```

profile of v0, /device:TPU:141, one launch (start us, length us, event | category | flops | bytes accessed | tf_op | source)
XLA Modules:
  0.0 195.3 jit_solution(15763246885604767730)
XLA Ops:
  0.0 0.0 copy-start
  0.8 1.0 fusion.17
  1.8 0.0 copy-start.5
  1.8 0.7 mul.110
  2.6 0.8 fusion.20
  3.4 0.0 copy-done.5
  3.4 0.8 pad_maximum_fusion
  4.2 2.1 %broadcast_in_dim.4 = bf16[64,2,2,4096]{3,2,1,0:T(2,128)(2,1)S(1)} broadcast(bf16[2,2,4096]{2,1,0:T(2,128)(2,1)S(1)} %pad_maximum_fusion), dimensions={1,2,3} | broadcast | bytes 2129920 | tf_op jit(solution)/shard_map/broadcast_in_dim | solution.py:17
  6.3 73.8 %all_to_all.10 = bf16[64,2,2,4096]{3,2,1,0:T(2,128)(2,1)S(1)} all-to-all(bf16[64,2,2,4096]{3,2,1,0:T(2,128)(2,1)S(1)} %broadcast_in_dim.4), channel_id=1, replica_groups=mesh['section'=16,'seqtp'=64] {'seqtp'}, dimensions={0} | all-to-all | bytes 4194304 | tf_op jit(solution)/shard_map/all_to_all | solution.py:17
  80.1 2.8 %fusion.24 = (bf16[1,64,2,4096]{3,2,0,1:T(2,128)(2,1)}, bf16[1,64,2,4096]{3,2,0,1:T(2,128)(2,1)}) fusion(bf16[2,64,2,4096]{3,2,0,1:T(2,128)(2,1)S(1)} %bitcast.52), kind=kLoop, calls=%fused_computation.34 | loop fusion | bytes 4194304 | tf_op jit(solution)/shard_map/slice | solution.py:62
  82.9 2.3 %squeeze.17 = bf16[128,4096]{1,0:T(8,128)(2,1)} reshape(bf16[1,64,2,4096]{3,2,0,1:T(2,128)(2,1)} %get-tuple-element.5) | data formatting | bytes 2097152 | tf_op jit(solution)/shard_map/squeeze | solution.py:62
  85.2 2.3 %squeeze.16 = bf16[128,4096]{1,0:T(8,128)(2,1)} reshape(bf16[1,64,2,4096]{3,2,0,1:T(2,128)(2,1)} %get-tuple-element.6) | data formatting | bytes 2097152 | tf_op jit(solution)/shard_map/squeeze | solution.py:63
  87.4 0.0 copy-start.1
  87.4 0.0 copy-start.2
  87.4 3.1 %fusion.26 = f32[128,384]{1,0:T(8,128)S(1)} fusion(bf16[128,4096]{1,0:T(8,128)(2,1)} %squeeze.17, bf16[4096,384]{1,0:T(8,128)(2,1)} %param.11), kind=kOutput, calls=%fused_computation.36 | convolution fusion | flops 402653184 | bytes 4390912 | tf_op jit(solution)/shard_map/dot_general | solution.py:61
  90.5 0.0 copy-done.1
  90.5 0.4 copy-done.2
  90.9 1.1 fusion.25
  92.0 0.0 copy-done
  92.0 5.3 %fusion.3 = f32[128,4096]{1,0:T(8,128)} fusion(bf16[4096,384]{1,0:T(8,128)(2,1)} %param.11, f32[128,384]{1,0:T(8,128)S(1)} %fusion.25, bf16[128,4096]{1,0:T(8,128)(2,1)} %squeeze.17, bf16[4096,384]{1,0:T(8,128)(2,1)S(1)} %copy-done, f32[128,384]{1,0:T(8,128)S(1)} %fusion.26), kind=kOutput, calls=%fused_computation.5 | convolution fusion | flops 805797888 | bytes 9830400 | tf_op jit(solution)/shard_map/dot_general | solution.py:48
  97.3 4.0 %convolution_add_fusion = f32[128,4096]{1,0:T(8,128)} fusion(f32[128,4096]{1,0:T(8,128)} %fusion.3, bf16[4096,384]{1,0:T(8,128)(2,1)S(1)} %copy-done, f32[128,384]{1,0:T(8,128)S(1)} %fusion.25, f32[128,384]{1,0:T(8,128)S(1)} %fusion.26), kind=kOutput, calls=%fused_computation | convolution fusion | flops 403472384 | bytes 7733248 | tf_op jit(solution)/shard_map/dot_general | solution.py:48
  101.3 3.5 %reshape.91 = f32[64,2,4096]{2,1,0:T(2,128)} reshape(f32[128,4096]{1,0:T(8,128)} %convolution_add_fusion) | data formatting | bytes 4194304 | tf_op jit(solution)/shard_map/reshape | solution.py:26
  104.8 0.0 copy-start.3
  104.8 0.0 copy-start.6
  104.8 0.0 copy-start.4
  104.8 78.1 %all_to_all.11 = f32[64,2,4096]{2,1,0:T(2,128)} all-to-all(f32[64,2,4096]{2,1,0:T(2,128)} %reshape.91), channel_id=1, replica_groups=mesh['section'=16,'seqtp'=64] {'seqtp'}, dimensions={0} | all-to-all | bytes 4194304 | tf_op jit(solution)/shard_map/all_to_all | solution.py:32
  182.9 2.2 %reduce_sum.28 = f32[2,4096]{1,0:T(2,128)S(1)} reduce(f32[64,2,4096]{2,1,0:T(2,128)} %all_to_all.11, f32[]{:T(128)} %constant.13.clone.1), dimensions={0}, to_apply=%region_1.2 | reduce | flops 516096 | bytes 2129924 | tf_op jit(solution)/shard_map/reduce_sum | solution.py:33
  185.1 0.0 copy-done.3
  185.1 0.0 copy-done.6
  185.1 0.2 fusion.13
  185.4 0.0 copy-done.4
  185.4 0.1 fusion.21
  185.5 8.3 %collective-permute-start = (bf16[2,4096]{1,0:T(2,128)(2,1)S(1)}, bf16[2,4096]{1,0:T(2,128)(2,1)S(1)}, u32[]{:S(2)}, u32[]{:S(2)}) collective-permute-start(bf16[2,4096]{1,0:T(2,128)(2,1)S(1)} %fusion.21), channel_id=1, source_target_pairs={{0,960},{64,0},{128,64},{192,128},{256,192},{320,256},{384,320},{4... | collective-permute-start | bytes 49160 | tf_op jit(solution)/shard_map/ppermute | solution.py:38
  193.8 0.8 collective-permute-done
  194.7 0.6 copy.10
  (2 shorter events, 0.0 us)
Async XLA Ops:
  0.0 92.0 %copy-start = (bf16[4096,384]{1,0:T(8,128)(2,1)S(1)}, bf16[4096,384]{1,0:T(8,128)(2,1)}, u32[]{:S(2)}) copy-start(bf16[4096,384]{1,0:T(8,128)(2,1)} %param.12) | copy-start | bytes 9437188
  1.8 1.6 copy-start.5
  87.4 3.1 %copy-start.1 = (bf16[128,4096]{1,0:T(8,128)(2,1)S(1)}, bf16[128,4096]{1,0:T(8,128)(2,1)}, u32[]{:S(2)}) copy-start(bf16[128,4096]{1,0:T(8,128)(2,1)} %squeeze.16) | copy-start | bytes 3145732
  87.4 3.5 %copy-start.2 = (bf16[384,4096]{1,0:T(8,128)(2,1)S(1)}, bf16[384,4096]{1,0:T(8,128)(2,1)}, u32[]{:S(2)}) copy-start(bf16[384,4096]{1,0:T(8,128)(2,1)} %param.13) | copy-start | bytes 9437188
  104.8 80.3 %copy-start.3 = (bf16[1,4,2,4096]{3,2,1,0:T(2,128)(2,1)S(1)}, bf16[1,4,2,4096]{3,2,1,0:T(2,128)(2,1)}, u32[]{:S(2)}) copy-start(bf16[1,4,2,4096]{3,2,1,0:T(2,128)(2,1)} %param.7) | copy-start | bytes 196612
  104.8 80.3 %copy-start.6 = (f32[2]{0:T(128)S(1)}, f32[2]{0:T(128)}, u32[]{:S(2)}) copy-start(f32[2]{0:T(128)} %copy-done.5) | copy-start | bytes 28
  104.8 80.6 %copy-start.4 = (bf16[1,2,4096]{2,1,0:T(2,128)(2,1)S(1)}, bf16[1,2,4096]{2,1,0:T(2,128)(2,1)}, u32[]{:S(2)}) copy-start(bf16[1,2,4096]{2,1,0:T(2,128)(2,1)} %param.8) | copy-start | bytes 49156
  185.5 9.2 %collective-permute-start = (bf16[2,4096]{1,0:T(2,128)(2,1)S(1)}, bf16[2,4096]{1,0:T(2,128)(2,1)S(1)}, u32[]{:S(2)}, u32[]{:S(2)}) collective-permute-start(bf16[2,4096]{1,0:T(2,128)(2,1)S(1)} %fusion.21), channel_id=1, source_target_pairs={{0,960},{64,0},{128,64},{192,128},{256,192},{320,256},{384,320},{4... | collective-permute-start | bytes 49160 | tf_op jit(solution)/shard_map/ppermute | solution.py:38
where the time goes:
time: 196 us; the launch traced here: 195 us
  blocking collectives  152 us (78%)
  local copies, waits for them, and re-layouts  14 us (7%)
  matrix products  13.4 us (7%)
  starting transfers between devices  8.35 us (4%)
  other arithmetic  5.89 us (3%)
    all_to_all x1, blocking collectives, sum_at_owner(): lax.all_to_all(blocks, axis, split_axis=0, concat_axis=0, tiled=True)  78.1 us
    all_to_all x1, blocking collectives, copy_for_each(): lax.all_to_all(jnp.broadcast_to(x[None], (length, *x.shape)), axis, 0, 0,...  73.8 us
    dot_general x3, matrix products, transposed(): lax.dot_general(left, weight, (((1,), (1,)), ((), ())), preferred_element...  10.4 us
    ppermute x1, starting transfers between devices, passed_along(): lax.ppermute(x, axis, [(i, (i + by) % length) for i in range(length)])  8.35 us
  transfers between devices with their start and end apart: 1, of which 1 were waited for; matrix products, arithmetic and copies ran while one was open for 0% of the time, Pallas kernels for 0%

commit v1 on v0

v1 whole, which is shorter than its diff:
```python
import jax
import jax.numpy as jnp
from jax import lax
from jax.experimental import pallas as pl
from jax.experimental.pallas import tpu as pltpu
from jax.sharding import PartitionSpec as P

EPS = 1e-05
MESH = pl.DeviceIdType.MESH
NX, NZ, NC = 4, 8, 2
J = 4
BF, F32 = jnp.bfloat16, jnp.float32
OTHERS = [(dx, dc) for dx in (2, 1, 3, 0) for dc in (0, 1) if (dx, dc) != (0, 0)]


def nt(left, right):
    return lax.dot_general(left, right, (((1,), (1,)), ((), ())), preferred_element_type=F32)


def kernel(
    saved_ref, cot_ref, slot_ref, gain_ref, wg_hbm, wu_hbm, wd_hbm, out_ref,
    wgu, wd, own, first, x_buf, gu, dh, dboth, y_send, pair_buf, total, hop_buf, hop_send,
    t_send, t_recv, dn, grad_buf,
    w_sem, a_send, a_recv, ring_send, ring_recv, sib_send, sib_recv,
    pair_send, pair_recv, red_send, red_recv, t_ssem, t_rsem, out_ssem, out_rsem,
):
    sect = lax.axis_index("section")
    seq = lax.axis_index("seqtp")
    n_sect = lax.axis_size("section")
    xh, z, c = seq // (NZ * NC), lax.rem(seq // NC, NZ), lax.rem(seq, NC)
    width = x_buf.shape[-1]
    hidden = wd.shape[0]

    def at(dx, dz, dc):
        x2 = lax.rem(xh + dx + NX, NX)
        z2 = lax.rem(z + dz + NZ, NZ)
        c2 = lax.rem(c + dc, NC)
        return (sect, (x2 * NZ + z2) * NC + c2)

    after = (lax.rem(sect + 1, n_sect), seq)
    before = (lax.rem(sect + n_sect - 1, n_sect), seq)
    partners = [at(dx, 0, dc) for dx, dc in OTHERS] + [at(0, 1, 0), at(0, -1, 0), after, before]

    barrier = pltpu.get_barrier_semaphore()
    for who in partners:
        pl.semaphore_signal(barrier, inc=1, device_id=who, device_id_type=MESH)

    loads = [
        pltpu.make_async_copy(wg_hbm, wgu.at[:, pl.ds(0, hidden)], w_sem.at[0]),
        pltpu.make_async_copy(wu_hbm, wgu.at[:, pl.ds(hidden, hidden)], w_sem.at[1]),
        pltpu.make_async_copy(wd_hbm, wd, w_sem.at[2]),
    ]
    for load in loads:
        load.start()

    gain_vec = gain_ref[...].astype(F32)
    behind = saved_ref[0, slot_ref[0]].astype(F32)
    recip = lax.rsqrt(jnp.mean(behind * behind, axis=-1, keepdims=True) + EPS)
    normed = (behind * recip * gain_vec).astype(BF)
    for k in range(2 * J):
        own[k, 0] = normed[:, k * width : (k + 1) * width]
        own[k, 1] = cot_ref[0, :, k * width : (k + 1) * width]

    pl.semaphore_wait(barrier, len(partners))

    def half(dc):
        return lax.rem(c + dc, NC) * J

    for j in range(J):
        for dx, dc in OTHERS:
            pltpu.make_async_remote_copy(
                own.at[half(dc) + j],
                first.at[j, ((NX - dx) % NX) * NC + dc],
                a_send, a_recv.at[j], at(dx, 0, dc), MESH,
            ).start()
        first[j, 0] = own[half(0) + j]

    def rows(dz):
        return pl.ds(pl.multiple_of(lax.rem(z + dz + NZ, NZ) * 16, 16), 16)

    def hops(j, d):
        return 4 if (j + d) % 2 == 0 else 3

    def ring(j, d, h):
        sgn = 1 - 2 * d
        block = x_buf.at[half(0) + j, :, rows(-sgn * (h - 1))]
        return pltpu.make_async_remote_copy(
            block, block, ring_send, ring_recv.at[j, d, h - 1], at(0, sgn, 0), MESH
        )

    def ring_arrival(j, d, h):
        sgn = 1 - 2 * d
        block = x_buf.at[half(0) + j, :, rows(-sgn * h)]
        return pltpu.make_async_remote_copy(
            block, block, ring_send, ring_recv.at[j, d, h - 1], at(0, sgn, 0), MESH
        )

    def share(j, dz):
        block = x_buf.at[half(0) + j, :, rows(dz)]
        pltpu.make_async_remote_copy(
            block, block, sib_send, sib_recv.at[j], at(0, 0, 1), MESH
        ).start()

    for j in range(J):
        arrived = first.at[j, pl.ds(1, 7)]
        pltpu.make_async_remote_copy(
            arrived, arrived, a_send, a_recv.at[j], at(0, 0, 1), MESH
        ).wait_recv()
        for a in range(2):
            parts = [
                first[j, dx * NC + lax.rem(c2 + c, NC), a].astype(F32)
                for dx in range(NX) for c2 in range(NC)
            ]
            x_buf[half(0) + j, a, rows(0), :] = jnp.concatenate(parts, axis=0).astype(BF)
        ring(j, 0, 1).start()
        ring(j, 1, 1).start()
        share(j, 0)

    gu[...] = jnp.zeros_like(gu)
    dh[...] = jnp.zeros_like(dh)

    def first_products(k):
        cols = pl.ds(pl.multiple_of(k * width, width), width)
        gu[...] += jnp.dot(x_buf[k, 0], wgu[cols, :], preferred_element_type=F32)
        dh[...] += nt(x_buf[k, 1], wd[:, cols])

    for h in range(1, 5):
        for j in range(J):
            for d in range(2):
                if h <= hops(j, d):
                    ring_arrival(j, d, h).wait_recv()
                    if h < hops(j, d):
                        ring(j, d, h + 1).start()
                    share(j, -(1 - 2 * d) * h)
            if h == 4:
                if j == 0:
                    for load in loads:
                        load.wait()
                first_products(half(0) + j)
                theirs = x_buf.at[half(1) + j]
                pltpu.make_async_remote_copy(
                    theirs, theirs, sib_send, sib_recv.at[j], at(0, 0, 1), MESH
                ).wait_recv()
                first_products(half(1) + j)

    gate, up, hid = gu[:, :hidden], gu[:, hidden:], dh[...]
    probe = jax.nn.sigmoid(gate)
    dboth[:, :hidden] = (hid * up * probe * (1.0 + gate * (1.0 - probe))).astype(BF)
    dboth[:, hidden:] = (hid * gate * probe).astype(BF)

    def second_product(k):
        return nt(dboth[...], wgu[pl.ds(pl.multiple_of(k * width, width), width), :])

    def reduce_hop(j, d, h, src):
        return pltpu.make_async_remote_copy(
            src, hop_buf.at[j, d, h - 1], red_send, red_recv.at[j, d, h - 1],
            at(0, 1 - 2 * d, 0), MESH,
        )

    def give(j):
        y_send[j] = second_product(half(1) + j).astype(BF)
        pltpu.make_async_remote_copy(
            y_send.at[j], pair_buf.at[j], pair_send, pair_recv.at[j], at(0, 0, 1), MESH
        ).start()

    def join(j):
        pltpu.make_async_remote_copy(
            y_send.at[j], pair_buf.at[j], pair_send, pair_recv.at[j], at(0, 0, 1), MESH
        ).wait_recv()
        total[j] += pair_buf[j].astype(F32)
        for d in range(2):
            sgn = 1 - 2 * d
            hop_send[j, d] = total[j, rows(sgn * hops(j, d)), :].astype(BF)
            reduce_hop(j, d, 1, hop_send.at[j, d]).start()

    def turn(j, h):
        for d in range(2):
            sgn = 1 - 2 * d
            last = hops(j, d)
            if h > last:
                continue
            reduce_hop(j, d, h, hop_buf.at[j, d, h - 1]).wait_recv()
            if h < last:
                hop_buf[j, d, h - 1] = (
                    hop_buf[j, d, h - 1].astype(F32) + total[j, rows(sgn * (last - h)), :]
                ).astype(BF)
                reduce_hop(j, d, h + 1, hop_buf.at[j, d, h - 1]).start()
        if h == 4:
            mine = total[j, rows(0), :]
            for d in range(2):
                mine = mine + hop_buf[j, d, hops(j, d) - 1].astype(F32)
            for dx in range(NX):
                for c2 in range(NC):
                    r = dx * 4 + c2 * 2
                    t_send[j, dx, c2] = mine[r : r + 2].astype(BF)
            for dx, dc in OTHERS:
                pltpu.make_async_remote_copy(
                    t_send.at[j, dx, lax.rem(c + dc, NC)],
                    t_recv.at[j, ((NX - dx) % NX) * NC + dc],
                    t_ssem, t_rsem.at[j], at(dx, 0, dc), MESH,
                ).start()

    give(0)
    total[0] = second_product(half(0))
    give(1)
    join(0)
    total[1] = second_product(half(0) + 1)
    give(2)
    join(1)
    total[2] = second_product(half(0) + 2)
    give(3)
    turn(0, 1)
    join(2)
    total[3] = second_product(half(0) + 3)
    turn(1, 1)
    join(3)
    for j, h in ((0, 2), (2, 1), (1, 2), (3, 1), (0, 3), (2, 2), (1, 3), (3, 2), (0, 4), (2, 3), (1, 4), (3, 3), (2, 4), (3, 4)):
        turn(j, h)

    for j in range(J):
        arrived = t_recv.at[j, pl.ds(1, 7)]
        pltpu.make_async_remote_copy(
            arrived, arrived, t_ssem, t_rsem.at[j], at(0, 0, 1), MESH
        ).wait_recv()
        mine = t_send[j, 0, c].astype(F32)
        for dx in range(1, NX):
            mine = mine + t_recv[j, dx * NC].astype(F32)
        theirs = t_recv[j, 1].astype(F32)
        for dx in range(1, NX):
            theirs = theirs + t_recv[j, dx * NC + 1].astype(F32)
        dn[half(0) + j] = mine
        dn[half(1) + j] = theirs

    d_normed = jnp.concatenate([dn[k] for k in range(2 * J)], axis=1)
    scaled = gain_vec * d_normed
    unit = saved_ref[0, slot_ref[0]].astype(F32) * recip
    grad = cot_ref[0].astype(F32) + recip * (
        scaled - unit * jnp.mean(scaled * unit, axis=-1, keepdims=True)
    )
    grad_buf[0] = grad.astype(BF)
    result = pltpu.make_async_remote_copy(grad_buf, out_ref, out_ssem, out_rsem, before, MESH)
    result.start()

    def drain(ref, sem):
        pltpu.make_async_copy(ref, ref, sem).wait()

    drain(first.at[:, pl.ds(1, 7)], a_send)
    drain(x_buf.at[pl.ds(0, J), :, pl.ds(0, 7 * 16)], ring_send)
    drain(x_buf.at[pl.ds(0, J)], sib_send)
    drain(pair_buf, pair_send)
    drain(hop_buf.at[:, pl.ds(0, 1)], red_send)
    drain(hop_buf.at[:, pl.ds(0, 1), pl.ds(0, 3)], red_send)
    drain(t_recv.at[:, pl.ds(1, 7)], t_ssem)
    result.wait()


def on_device(saved_in, grad_in, slot_table, gain, w_gate, w_up, w_down):
    d, hidden = w_gate.shape
    width = d // (2 * J)
    tokens = NX * NZ * NC * 2
    vmem = pl.BlockSpec(memory_space=pltpu.VMEM)
    hbm = pl.BlockSpec(memory_space=pl.ANY)
    dma = pltpu.SemaphoreType.DMA
    return pl.pallas_call(
        kernel,
        out_shape=jax.ShapeDtypeStruct(grad_in.shape, BF),
        in_specs=[vmem, vmem, pl.BlockSpec(memory_space=pltpu.SMEM), vmem, hbm, hbm, hbm],
        out_specs=hbm,
        scratch_shapes=[
            pltpu.VMEM((d, 2 * hidden), BF),
            pltpu.VMEM((hidden, d), BF),
            pltpu.VMEM((2 * J, 2, 2, width), BF),
            pltpu.VMEM((J, NX * NC, 2, 2, width), BF),
            pltpu.VMEM((2 * J, 2, tokens, width), BF),
            pltpu.VMEM((tokens, 2 * hidden), F32),
            pltpu.VMEM((tokens, hidden), F32),
            pltpu.VMEM((tokens, 2 * hidden), BF),
            pltpu.VMEM((J, tokens, width), BF),
            pltpu.VMEM((J, tokens, width), BF),
            pltpu.VMEM((J, tokens, width), F32),
            pltpu.VMEM((J, 2, 4, 16, width), BF),
            pltpu.VMEM((J, 2, 16, width), BF),
            pltpu.VMEM((J, NX, NC, 2, width), BF),
            pltpu.VMEM((J, NX * NC, 2, width), BF),
            pltpu.VMEM((2 * J, 2, width), F32),
            pltpu.VMEM(grad_in.shape, BF),
            dma((3,)), dma, dma((J,)), dma, dma((J, 2, 4)), dma, dma((J,)),
            dma, dma((J,)), dma, dma((J, 2, 4)), dma, dma((J,)), dma, dma,
        ],
        compiler_params=pltpu.CompilerParams(
            collective_id=0, has_side_effects=True, vmem_limit_bytes=40 * 1024 * 1024
        ),
    )(saved_in, grad_in, slot_table, gain, w_gate, w_up, w_down)


def solution(mesh):
    return jax.shard_map(
        on_device,
        mesh=mesh,
        in_specs=(
            P("section", None, "seqtp", None),
            P("section", "seqtp", None),
            P("section"),
            P("section", None),
            P(None, "seqtp"),
            P(None, "seqtp"),
            P("seqtp", None),
        ),
        out_specs=P("section", "seqtp", None),
        check_vma=False,
    )
```

time: 196 us -> 80.5 us (0.41)
  the two profiles are of different devices: /device:TPU:141 before, /device:TPU:51 now
where the time goes in v1:
time: 80.5 us; the launch traced here: 79.5 us
  Pallas kernels  70.3 us (87%)
  local copies, waits for them, and re-layouts  8.54 us (11%)
    pallas_call x1, Pallas kernels, on_device(): pl.pallas_call(kernel, out_shape=jax.ShapeDtypeStruct(grad_in.shape, BF),...  70.3 us
    unnamed x13, local copies, waits for them, and re-layouts  8.54 us

profile of v1, /device:TPU:51, one launch (start us, length us, event | category | flops | bytes accessed | tf_op | source)
XLA Modules:
  0.0 79.5 jit_solution(6799746248786004548)
XLA Ops:
  0.7 0.0 copy-start
  0.7 1.9 %copy-done = bf16[4096,384]{1,0:T(8,128)(2,1)S(1)} copy-done((bf16[4096,384]{1,0:T(8,128)(2,1)S(1)}, bf16[4096,384]{1,0:T(8,128)(2,1)}, u32[]{:S(2)}) %copy-start) | copy-done | bytes 3145752
  2.5 0.0 copy-start.1
  2.5 1.9 %copy-done.1 = bf16[4096,384]{1,0:T(8,128)(2,1)S(1)} copy-done((bf16[4096,384]{1,0:T(8,128)(2,1)S(1)}, bf16[4096,384]{1,0:T(8,128)(2,1)}, u32[]{:S(2)}) %copy-start.1) | copy-done | bytes 3145752
  4.4 0.0 copy-start.2
  4.4 1.9 %copy-done.2 = bf16[384,4096]{1,0:T(8,128)(2,1)S(1)} copy-done((bf16[384,4096]{1,0:T(8,128)(2,1)S(1)}, bf16[384,4096]{1,0:T(8,128)(2,1)}, u32[]{:S(2)}) %copy-start.2) | copy-done | bytes 3145752
  6.3 0.0 copy-start.3
  6.3 0.8 %copy-done.3 = bf16[1,4,2,4096]{3,2,1,0:T(2,128)(2,1)S(1)} copy-done((bf16[1,4,2,4096]{3,2,1,0:T(2,128)(2,1)S(1)}, bf16[1,4,2,4096]{3,2,1,0:T(2,128)(2,1)}, u32[]{:S(2)}) %copy-start.3) | copy-done | bytes 65560
  7.2 0.0 copy-start.4
  7.2 0.7 copy-done.4
  7.9 0.0 copy-start.5
  7.9 0.7 copy-done.5
  8.6 70.3 %shard_map.73 = bf16[1,2,4096]{2,1,0:T(2,128)(2,1)S(1)} custom-call(bf16[1,4,2,4096]{3,2,1,0:T(2,128)(2,1)S(1)} %copy-done.3, bf16[1,2,4096]{2,1,0:T(2,128)(2,1)S(1)} %copy-done.4, s32[1]{0:T(128)S(6)} %copy.9.slot_ref, bf16[1,4096]{1,0:T(2,128)(2,1)S(1)} %copy-done.5, bf16[4096,384]{1,0:T(8,128)(2,1)S(1)} %copy-done, bf16[4096,384]{1,0:T(8,128)(2,1)S(1)} %copy-done.1, ...), custom_call_target="tpu_custom_call" | custom-call | tf_op jit(solution)/shard_map/pallas_call | solution.py:264
  78.9 0.6 copy.10
Async XLA Ops:
  0.7 1.9 %copy-start = (bf16[4096,384]{1,0:T(8,128)(2,1)S(1)}, bf16[4096,384]{1,0:T(8,128)(2,1)}, u32[]{:S(2)}) copy-start(bf16[4096,384]{1,0:T(8,128)(2,1)} %wg_hbm.1) | copy-start | bytes 9437188
  2.5 1.9 %copy-start.1 = (bf16[4096,384]{1,0:T(8,128)(2,1)S(1)}, bf16[4096,384]{1,0:T(8,128)(2,1)}, u32[]{:S(2)}) copy-start(bf16[4096,384]{1,0:T(8,128)(2,1)} %wu_hbm.1) | copy-start | bytes 9437188
  4.4 1.9 %copy-start.2 = (bf16[384,4096]{1,0:T(8,128)(2,1)S(1)}, bf16[384,4096]{1,0:T(8,128)(2,1)}, u32[]{:S(2)}) copy-start(bf16[384,4096]{1,0:T(8,128)(2,1)} %wd_hbm.1) | copy-start | bytes 9437188
  6.3 0.8 %copy-start.3 = (bf16[1,4,2,4096]{3,2,1,0:T(2,128)(2,1)S(1)}, bf16[1,4,2,4096]{3,2,1,0:T(2,128)(2,1)}, u32[]{:S(2)}) copy-start(bf16[1,4,2,4096]{3,2,1,0:T(2,128)(2,1)} %saved_ref.1) | copy-start | bytes 196612
  7.2 0.7 copy-start.4
  7.9 0.7 copy-start.5

commit v2 on v1

v2 whole, which is shorter than its diff:
```python
import jax
import jax.numpy as jnp
from jax import lax
from jax.experimental import pallas as pl
from jax.experimental.pallas import tpu as pltpu
from jax.sharding import PartitionSpec as P

EPS = 1e-05
MESH = pl.DeviceIdType.MESH
NX, NZ, NC = 4, 8, 2
J = 4
G = 2
PER = J // G
BF, F32 = jnp.bfloat16, jnp.float32
ALL = [(dx, dc) for dx in (2, 1, 3, 0) for dc in (0, 1)]
BARRIER_Z = (1, -1)
ORDER = (
    (1, 2, 7, 6, 3, 5, 4),
    (1, 7, 2, 6, 3, 5, 4),
    (7, 1, 2, 6, 3, 5, 4),
    (7, 6, 1, 2, 5, 3, 4),
    (7, 6, 1, 5, 2, 3, 4),
    (7, 6, 1, 5, 2, 3, 4),
    (7, 1, 6, 2, 5, 3, 4),
    (1, 7, 2, 6, 3, 5, 4),
)
OTHERS = [(dx, dc) for dx in (2, 1, 3, 0) for dc in (0, 1) if (dx, dc) != (0, 0)]


def nt(left, right):
    return lax.dot_general(left, right, (((1,), (1,)), ((), ())), preferred_element_type=F32)


def kernel(
    saved_hbm, cot_hbm, slot_ref, gain_hbm, wg_hbm, wu_hbm, wd_hbm, out_ref,
    saved, cot, gain, picked, saved_next, cot_next, gain_next,
    wgu, wd, own, first, x_buf, gu, dh, dboth, y_send, pair_buf, total, r_send, r_recv, m_send,
    t_send, t_recv, dn,
    in_sem, w_sem, next_send, next_recv, a_send, a_recv, z_send, z_recv, sib_send, sib_recv,
    pair_send, pair_recv, red_send, red_recv, t_ssem, t_rsem,
):
    sect = lax.axis_index("section")
    seq = lax.axis_index("seqtp")
    n_sect = lax.axis_size("section")
    xh, z, c = seq // (NZ * NC), lax.rem(seq // NC, NZ), lax.rem(seq, NC)
    width = x_buf.shape[-1]
    hidden = wd.shape[0]

    def at(dx, dz, dc, ds=0):
        x2 = lax.rem(xh + dx + NX, NX)
        z2 = lax.rem(z + dz + NZ, NZ)
        c2 = lax.rem(c + dc, NC)
        return (lax.rem(sect + ds + n_sect, n_sect), (x2 * NZ + z2) * NC + c2)

    partners = [at(dx, 0, dc) for dx, dc in OTHERS]
    partners += [at(0, dz, 0) for dz in BARRIER_Z]
    partners += [at(dx, 0, dc, ds) for ds in (1, -1) for dx, dc in ALL]

    inputs = [
        pltpu.make_async_copy(saved_hbm, saved, in_sem.at[0]),
        pltpu.make_async_copy(cot_hbm, cot, in_sem.at[1]),
        pltpu.make_async_copy(gain_hbm, gain, in_sem.at[2]),
    ]
    loads = [
        pltpu.make_async_copy(wg_hbm, wgu.at[:, pl.ds(0, hidden)], w_sem.at[0]),
        pltpu.make_async_copy(wu_hbm, wgu.at[:, pl.ds(hidden, hidden)], w_sem.at[1]),
        pltpu.make_async_copy(wd_hbm, wd, w_sem.at[2]),
    ]
    for load in inputs:
        load.start()
    barrier = pltpu.get_barrier_semaphore()
    for who in partners:
        pl.semaphore_signal(barrier, inc=1, device_id=who, device_id_type=MESH)
    for load in loads:
        load.start()
    for load in inputs:
        load.wait()

    def recip_of(values):
        return lax.rsqrt(jnp.mean(values * values, axis=-1, keepdims=True) + EPS)

    picked[...] = saved[0, slot_ref[0]]
    behind = picked[...].astype(F32)
    normed = (behind * recip_of(behind) * gain[...].astype(F32)).astype(BF)
    for k in range(2 * J):
        own[k, 0] = normed[:, k * width : (k + 1) * width]
        own[k, 1] = cot[0, :, k * width : (k + 1) * width]

    pl.semaphore_wait(barrier, len(partners))

    def half(dc):
        return lax.rem(c + dc, NC) * J

    for g in range(G):
        for dx, dc in OTHERS:
            pltpu.make_async_remote_copy(
                own.at[pl.ds(half(dc) + g * PER, PER)],
                first.at[g, ((NX - dx) % NX) * NC + dc],
                a_send, a_recv.at[g], at(dx, 0, dc), MESH,
            ).start()
        for i in range(PER):
            first[g, 0, i] = own[half(0) + g * PER + i]

    def ahead(i, src, dst):
        return pltpu.make_async_remote_copy(
            src, dst, next_send.at[i], next_recv.at[i], at(0, 0, 0, -1), MESH
        )

    handed = [ahead(0, picked, saved_next), ahead(1, cot, cot_next), ahead(2, gain, gain_next)]
    for copy in handed:
        copy.start()

    def rows(dz):
        return pl.ds(pl.multiple_of(lax.rem(z + dz + NZ, NZ) * 16, 16), 16)

    def push(j, origin, dz):
        block = x_buf.at[half(0) + j, :, rows(origin)]
        return pltpu.make_async_remote_copy(
            block, block, z_send, z_recv.at[j, lax.rem(origin - dz + NZ, NZ)], at(0, dz, 0), MESH
        )

    def arrival(j, origin):
        block = x_buf.at[half(0) + j, :, rows(origin)]
        pltpu.make_async_remote_copy(
            block, block, z_send, z_recv.at[j, origin], at(0, 1, 0), MESH
        ).wait_recv()

    def share(j, dz):
        block = x_buf.at[half(0) + j, :, rows(dz)]
        pltpu.make_async_remote_copy(
            block, block, sib_send, sib_recv.at[j], at(0, 0, 1), MESH
        ).start()

    for j in range(J):
        if j % PER == 0:
            arrived = first.at[j // PER, pl.ds(1, 7)]
            pltpu.make_async_remote_copy(
                arrived, arrived, a_send, a_recv.at[j // PER], at(0, 0, 1), MESH
            ).wait_recv()
        for a in range(2):
            parts = [
                first[j // PER, dx * NC + lax.rem(c2 + c, NC), j % PER, a].astype(F32)
                for dx in range(NX) for c2 in range(NC)
            ]
            x_buf[half(0) + j, a, rows(0), :] = jnp.concatenate(parts, axis=0).astype(BF)
        for dz in (1, -1):
            push(j, 0, dz).start()
        share(j, 0)

    gu[...] = jnp.zeros_like(gu)
    dh[...] = jnp.zeros_like(dh)

    def first_products(k):
        cols = pl.ds(pl.multiple_of(k * width, width), width)
        gu[...] += jnp.dot(x_buf[k, 0], wgu[cols, :], preferred_element_type=F32)
        dh[...] += nt(x_buf[k, 1], wd[:, cols])

    def handle(j, r):
        arrival(j, r)
        plus = r > NZ // 2
        end = (r == NZ // 2) | (r == (NZ // 2 + 1 if j % 2 else NZ // 2 - 1))

        @pl.when(jnp.logical_not(end))
        def _():
            push(j, r, jnp.where(plus, 1, -1)).start()

        share(j, r)

    for t in range(NZ - 1):
        r = sum(jnp.where(z == i, ORDER[i][t], 0) for i in range(NZ))
        for j in range(J):
            handle(j, r)
            if t == NZ - 2:
                if j == 0:
                    for load in loads:
                        load.wait()
                first_products(half(0) + j)
                theirs = x_buf.at[half(1) + j]
                pltpu.make_async_remote_copy(
                    theirs, theirs, sib_send, sib_recv.at[j], at(0, 0, 1), MESH
                ).wait_recv()
                first_products(half(1) + j)

    gate, up, hid = gu[:, :hidden], gu[:, hidden:], dh[...]
    probe = jax.nn.sigmoid(gate)
    dboth[:, :hidden] = (hid * up * probe * (1.0 + gate * (1.0 - probe))).astype(BF)
    dboth[:, hidden:] = (hid * gate * probe).astype(BF)

    def second_product(k):
        return nt(dboth[...], wgu[pl.ds(pl.multiple_of(k * width, width), width), :])

    def pair_copy(j):
        return pltpu.make_async_remote_copy(
            y_send.at[j], pair_buf.at[j], pair_send, pair_recv.at[j], at(0, 0, 1), MESH
        )

    def give(j):
        y_send[j] = second_product(half(1) + j).astype(BF)
        pair_copy(j).start()

    def reduce_copy(j, slot, src, dz):
        return pltpu.make_async_remote_copy(
            src, r_recv.at[j, slot], red_send, red_recv.at[j, slot], at(0, dz, 0), MESH
        )

    def landed(j, slot):
        reduce_copy(j, slot, r_recv.at[j, slot], 1).wait_recv()
        return r_recv[j, slot].astype(F32)

    def far(j):
        return 1 if j % 2 == 0 else -1

    def join(j):
        summed = second_product(half(0) + j)
        pair_copy(j).wait_recv()
        summed = summed + pair_buf[j].astype(F32)
        total[j] = summed
        r_send[j] = summed.astype(BF)
        reduce_copy(j, 2, r_send.at[j, rows(4)], 2 * far(j)).start()
        reduce_copy(j, 0, r_send.at[j, rows(3)], 1).start()
        reduce_copy(j, 1, r_send.at[j, rows(-3)], -1).start()
        reduce_copy(j, 3, r_send.at[j, rows(1)], 1).start()
        reduce_copy(j, 4, r_send.at[j, rows(-1)], -1).start()

    def merge(j):
        more = landed(j, 2)
        for i, sgn in ((0, 1), (1, -1)):
            block = total[j, rows(2 * sgn), :] + landed(j, i)
            if sgn == far(j):
                block = block + more
            m_send[j, i] = block.astype(BF)
            reduce_copy(j, 5 + i, m_send.at[j, i], 2 * sgn).start()

    def finish(j):
        block = total[j, rows(0), :]
        for slot in (3, 4, 5, 6):
            block = block + landed(j, slot)
        for dx in range(NX):
            for c2 in range(NC):
                r = dx * 4 + c2 * 2
                t_send[dx, c2, j] = block[r : r + 2].astype(BF)
        g = j // PER
        if j % PER == PER - 1:
            for dx, dc in ALL:
                pltpu.make_async_remote_copy(
                    t_send.at[dx, lax.rem(c + dc, NC), pl.ds(g * PER, PER)],
                    t_recv.at[g, ((NX - dx) % NX) * NC + dc],
                    t_ssem, t_rsem.at[g], at(dx, 0, dc, -1), MESH,
                ).start()

    give(0)
    give(1)
    join(0)
    give(2)
    join(1)
    give(3)
    join(2)
    join(3)
    for j in range(J):
        merge(j)
    for j in range(J):
        finish(j)

    for copy in handed:
        copy.wait_recv()
    behind = saved_next[...].astype(F32)
    recip = recip_of(behind)
    unit = behind * recip
    for j in range(J):
        g, i = j // PER, j % PER
        if i == 0:
            pltpu.make_async_remote_copy(
                t_recv.at[g], t_recv.at[g], t_ssem, t_rsem.at[g], at(0, 0, 1), MESH
            ).wait_recv()
        for dc in range(NC):
            part = t_recv[g, dc, i].astype(F32)
            for dx in range(1, NX):
                part = part + t_recv[g, dx * NC + dc, i].astype(F32)
            dn[half(dc) + j] = part

    d_normed = jnp.concatenate([dn[k] for k in range(2 * J)], axis=1)
    scaled = gain_next[...].astype(F32) * d_normed
    grad = cot_next[0].astype(F32) + recip * (
        scaled - unit * jnp.mean(scaled * unit, axis=-1, keepdims=True)
    )
    out_ref[0] = grad.astype(BF)

    def drain(ref, sem):
        pltpu.make_async_copy(ref, ref, sem).wait()

    for copy in handed:
        copy.wait_send()
    drain(first.at[:, pl.ds(1, 7)], a_send)
    drain(x_buf.at[pl.ds(0, J), :, pl.ds(0, 7 * 16)], z_send)
    drain(x_buf.at[pl.ds(0, J)], sib_send)
    drain(pair_buf, pair_send)
    drain(r_recv, red_send)
    drain(t_recv, t_ssem)


def on_device(saved_in, grad_in, slot_table, gain, w_gate, w_up, w_down):
    d, hidden = w_gate.shape
    width = d // (2 * J)
    tokens = NX * NZ * NC * 2
    hbm = pl.BlockSpec(memory_space=pltpu.HBM)
    dma = pltpu.SemaphoreType.DMA
    row = (saved_in.shape[2], d)
    return pl.pallas_call(
        kernel,
        out_shape=jax.ShapeDtypeStruct(grad_in.shape, BF),
        in_specs=[hbm, hbm, pl.BlockSpec(memory_space=pltpu.SMEM), hbm, hbm, hbm, hbm],
        out_specs=pl.BlockSpec(memory_space=pltpu.VMEM),
        scratch_shapes=[
            pltpu.VMEM(saved_in.shape, BF),
            pltpu.VMEM(grad_in.shape, BF),
            pltpu.VMEM(gain.shape, BF),
            pltpu.VMEM(row, BF),
            pltpu.VMEM(row, BF),
            pltpu.VMEM(grad_in.shape, BF),
            pltpu.VMEM(gain.shape, BF),
            pltpu.VMEM((d, 2 * hidden), BF),
            pltpu.VMEM((hidden, d), BF),
            pltpu.VMEM((2 * J, 2, 2, width), BF),
            pltpu.VMEM((G, NX * NC, PER, 2, 2, width), BF),
            pltpu.VMEM((2 * J, 2, tokens, width), BF),
            pltpu.VMEM((tokens, 2 * hidden), F32),
            pltpu.VMEM((tokens, hidden), F32),
            pltpu.VMEM((tokens, 2 * hidden), BF),
            pltpu.VMEM((J, tokens, width), BF),
            pltpu.VMEM((J, tokens, width), BF),
            pltpu.VMEM((J, tokens, width), F32),
            pltpu.VMEM((J, tokens, width), BF),
            pltpu.VMEM((J, NZ - 1, 16, width), BF),
            pltpu.VMEM((J, 2, 16, width), BF),
            pltpu.VMEM((NX, NC, J, 2, width), BF),
            pltpu.VMEM((G, NX * NC, PER, 2, width), BF),
            pltpu.VMEM((2 * J, 2, width), F32),
            dma((3,)), dma((3,)), dma((3,)), dma((3,)),
            dma, dma((G,)), dma, dma((J, NZ)), dma, dma((J,)),
            dma, dma((J,)), dma, dma((J, NZ - 1)), dma, dma((G,)),
        ],
        compiler_params=pltpu.CompilerParams(
            collective_id=0, has_side_effects=True, vmem_limit_bytes=60 * 1024 * 1024
        ),
    )(saved_in, grad_in, slot_table, gain, w_gate, w_up, w_down)


def solution(mesh):
    return jax.shard_map(
        on_device,
        mesh=mesh,
        in_specs=(
            P("section", None, "seqtp", None),
            P("section", "seqtp", None),
            P("section"),
            P("section", None),
            P(None, "seqtp"),
            P(None, "seqtp"),
            P("seqtp", None),
        ),
        out_specs=P("section", "seqtp", None),
        check_vma=False,
    )
```

time: 80.5 us -> 65.2 us (0.81)
  Pallas kernels: 70.3 us -> 63 us
  local copies, waits for them, and re-layouts: 8.54 us -> 1.34 us
    pallas_call x1, Pallas kernels: 70.3 us -> 63 us  [on_device(): pl.pallas_call(kernel, out_shape=jax.ShapeDtypeStruct(grad_in.shape, BF),...]
    unnamed x13 -> x1, local copies, waits for them, and re-layouts: 8.54 us -> 1.34 us
where the time goes in v2:
time: 65.2 us; the launch traced here: 65 us
  Pallas kernels  63 us (97%)
  local copies, waits for them, and re-layouts  1.34 us (2%)
  between operations  0.66 us (1%)
    pallas_call x1, Pallas kernels, on_device(): pl.pallas_call(kernel, out_shape=jax.ShapeDtypeStruct(grad_in.shape, BF),...  63 us
    unnamed x1, local copies, waits for them, and re-layouts  1.34 us

profile of v2, /device:TPU:51, one launch (start us, length us, event | category | flops | bytes accessed | tf_op | source)
XLA Modules:
  0.0 65.0 jit_solution(8468070775446684017)
XLA Ops:
  0.7 63.0 %shard_map.73 = bf16[1,2,4096]{2,1,0:T(2,128)(2,1)} custom-call(bf16[1,4,2,4096]{3,2,1,0:T(2,128)(2,1)} %saved_hbm.1, bf16[1,2,4096]{2,1,0:T(2,128)(2,1)} %cot_hbm.1, s32[1]{0:T(128)S(6)} %copy.9.slot_ref, bf16[1,4096]{1,0:T(2,128)(2,1)} %gain_hbm.1, bf16[4096,384]{1,0:T(8,128)(2,1)} %wg_hbm.1, bf16[4096,384]{1,0:T(8,128)(2,1)} %wu_hbm.1, ...), custom_call_target="tpu_custom_call" | custom-call | tf_op jit(solution)/shard_map/pallas_call | solution.py:308
  63.7 1.3 %copy.10 = bf16[1,2,4096]{2,1,0:T(2,128)(2,1)} copy(bf16[1,2,4096]{2,1,0:T(2,128)(2,1)} %shard_map.73) | data formatting | bytes 32768

commit v3 on v2

--- a/solution.py
+++ b/solution.py
@@ -9,7 +9,7 @@
 MESH = pl.DeviceIdType.MESH
 NX, NZ, NC = 4, 8, 2
 J = 4
-G = 2
+G = 4
 PER = J // G
 BF, F32 = jnp.bfloat16, jnp.float32
 ALL = [(dx, dc) for dx in (2, 1, 3, 0) for dc in (0, 1)]
@@ -145,6 +145,7 @@
             x_buf[half(0) + j, a, rows(0), :] = jnp.concatenate(parts, axis=0).astype(BF)
         for dz in (1, -1):
             push(j, 0, dz).start()
+    for j in range(J):
         share(j, 0)
 
     gu[...] = jnp.zeros_like(gu)
@@ -250,10 +251,10 @@
 
     give(0)
     give(1)
+    give(2)
     join(0)
-    give(2)
+    give(3)
     join(1)
-    give(3)
     join(2)
     join(3)
     for j in range(J):

time: 65.2 us -> 64.5 us (0.989)
  Pallas kernels: 63 us -> 62.3 us
    pallas_call x1, Pallas kernels: 63 us -> 62.3 us  [on_device(): pl.pallas_call(kernel, out_shape=jax.ShapeDtypeStruct(grad_in.shape, BF),...]
where the time goes in v3:
time: 64.5 us; the launch traced here: 64.3 us
  Pallas kernels  62.3 us (97%)
  local copies, waits for them, and re-layouts  1.34 us (2%)
  between operations  0.66 us (1%)
    pallas_call x1, Pallas kernels, on_device(): pl.pallas_call(kernel, out_shape=jax.ShapeDtypeStruct(grad_in.shape, BF),...  62.3 us
    unnamed x1, local copies, waits for them, and re-layouts  1.34 us

profile of v3, /device:TPU:51, one launch (start us, length us, event | category | flops | bytes accessed | tf_op | source)
XLA Modules:
  0.0 64.3 jit_solution(15852669464646302362)
XLA Ops:
  0.7 62.3 %shard_map.73 = bf16[1,2,4096]{2,1,0:T(2,128)(2,1)} custom-call(bf16[1,4,2,4096]{3,2,1,0:T(2,128)(2,1)} %saved_hbm.1, bf16[1,2,4096]{2,1,0:T(2,128)(2,1)} %cot_hbm.1, s32[1]{0:T(128)S(6)} %copy.9.slot_ref, bf16[1,4096]{1,0:T(2,128)(2,1)} %gain_hbm.1, bf16[4096,384]{1,0:T(8,128)(2,1)} %wg_hbm.1, bf16[4096,384]{1,0:T(8,128)(2,1)} %wu_hbm.1, ...), custom_call_target="tpu_custom_call" | custom-call | tf_op jit(solution)/shard_map/pallas_call | solution.py:309
  63.0 1.3 %copy.10 = bf16[1,2,4096]{2,1,0:T(2,128)(2,1)} copy(bf16[1,2,4096]{2,1,0:T(2,128)(2,1)} %shard_map.73) | data formatting | bytes 32768
